TPU v7x, 512 devices: a whole 4x8x8 slice. The times are simulated.
512 devices in a mesh: ent: 128 (over y, z, core), rep: 4 (over x).
Axes of the slice: x: 4, y: 8, z: 8, core: 2. Of those that a mesh axis runs over, the one named last changes fastest.
Arguments:
- entity_table: float32 [65536, 200], P('ent'), may hold values from -6 to 6
- relation_table: bfloat16 [822, 200], replicated, may hold values from -12 to 12
- filters: float32 [32, 9], replicated, may hold values from -2 to 2
- projection: bfloat16 [9728, 200], replicated, may hold values from -0.0625 to 0.0625
- request_owner: int32 [163840, 1], P(('ent', 'rep')), may hold values from 0 to 127; in each aligned block of 320 rows (0 to 319, 320 to 639, ...) at most 4 rows name the same one
- request_row: int32 [163840], P(('ent', 'rep')), may hold values from 0 to 511
- relation_id: int32 [65536], P(('ent', 'rep')), may hold values from 0 to 821
- rare_flag: int32 [65536], P('ent'), may hold values 0 or 1
- running_norm: float32 [], replicated, may hold values from 2 to 6
Outputs:
- new_table: float32 [65536, 200], P('ent')
- filter_grad: float32 [32, 9], replicated
Inputs may be any that keep to these rules, and one draw needn't show every extreme that they name: `request_owner`: among the requests of one device no owner shard is named more than 4 times, a bound that some block reaches.
All inputs are finite; a program needn't handle non-finite values. No bound on the sum of `rare_flag` on one device may be relied on, other than what follows from the above.
Results may differ from a plain program's by a relative error of at most 0.002.
Values sent between devices are 32-bit elements; how exact they have to be, the bound alone decides.
A program may use at most 64 MiB of HBM per device.

v0:
```python
import jax
import jax.numpy as jnp
from jax import lax
from jax.sharding import PartitionSpec as P

D = 200
ROWS = 20
learn_rate = 0.5
norm_eps = 1e-06


def conv_act(head_rows, rel_rows, filters):
    count = head_rows.shape[0]
    stacked = jnp.concatenate(
        [head_rows.reshape(count, ROWS, D // ROWS), rel_rows.reshape(count, ROWS, D // ROWS)],
        axis=1,
    )[:, None]
    kernel = filters.reshape(filters.shape[0], 1, 3, 3)
    conv_out = lax.conv_general_dilated(
        stacked, kernel, (1, 1), "VALID", precision=lax.Precision.HIGHEST
    )
    return jax.nn.silu(conv_out).reshape(count, -1)


def block_step(row_values, rel_rows, filters, projection, batch_rows, neg_count):
    head_rows = row_values[:batch_rows]
    pos_rows = row_values[batch_rows : 2 * batch_rows]
    neg_rows = row_values[2 * batch_rows :]
    activated, pullback = jax.vjp(
        lambda head_part, filt_part: conv_act(head_part, rel_rows, filt_part), head_rows, filters
    )
    features = activated.astype(jnp.bfloat16)
    projected = jnp.dot(features, projection, preferred_element_type=jnp.float32)
    sig_proj = jax.nn.sigmoid(projected)
    hidden = projected * sig_proj
    score_pos = jnp.sum(hidden * pos_rows, 1)
    score_neg = jnp.dot(hidden, neg_rows.T, precision=lax.Precision.HIGHEST)
    grad_pos = -jax.nn.sigmoid(-score_pos)
    grad_neg = jax.nn.sigmoid(score_neg) / neg_count
    pos_grad_rows = grad_pos[:, None] * hidden
    neg_grad_rows = jnp.dot(grad_neg.T, hidden, precision=lax.Precision.HIGHEST)
    grad_hidden = grad_pos[:, None] * pos_rows + jnp.dot(
        grad_neg, neg_rows, precision=lax.Precision.HIGHEST
    )
    grad_proj = (grad_hidden * sig_proj * (1.0 + projected * (1.0 - sig_proj))).astype(jnp.bfloat16)
    grad_feat = lax.dot_general(
        grad_proj, projection, (((1,), (1,)), ((), ())), preferred_element_type=jnp.float32
    )
    head_grad_rows, filter_part = pullback(grad_feat)
    return (jnp.concatenate([head_grad_rows, pos_grad_rows, neg_grad_rows], axis=0), filter_part)


def body(
    entity_table,
    relation_table,
    filters,
    projection,
    request_owner,
    request_row,
    relation_id,
    rare_flag,
    running_norm,
):
    ent_count = lax.axis_size("ent")
    rep_count = lax.axis_size("rep")
    req_count = request_row.shape[0]
    batch_rows = relation_id.shape[0]
    neg_count = req_count - 2 * batch_rows
    width = entity_table.shape[1]
    slots_each = max(2, 3 * req_count // (2 * ent_count) + 1)
    owner_shard = request_owner[:, 0]
    onehot = (owner_shard[:, None] == jnp.arange(ent_count, dtype=jnp.int32)[None, :]).astype(
        jnp.int32
    )
    slot_index = jnp.sum(jnp.cumsum(onehot, 0) * onehot, 1) - 1
    slot_place = owner_shard * slots_each + slot_index
    send_ids = (
        jnp.zeros((ent_count * slots_each,), jnp.int32)
        .at[slot_place]
        .set(request_row)
        .reshape(ent_count, slots_each)
    )
    wanted = lax.all_to_all(send_ids, "ent", split_axis=0, concat_axis=0, tiled=True)
    found_rows = entity_table[wanted]
    fetched = lax.all_to_all(found_rows, "ent", split_axis=0, concat_axis=0, tiled=True)
    row_values = fetched.reshape(-1, width)[slot_place]
    rel_rows = relation_table[relation_id].astype(jnp.float32)
    grads, filter_part = block_step(
        row_values, rel_rows, filters, projection, batch_rows, neg_count
    )
    send_grads = (
        jnp.zeros((ent_count * slots_each, width), jnp.float32)
        .at[slot_place]
        .set(grads)
        .reshape(ent_count, slots_each, width)
    )
    received = lax.all_to_all(send_grads, "ent", split_axis=0, concat_axis=0, tiled=True)
    all_ids = lax.all_gather(wanted, "rep", axis=0, tiled=True)
    all_grads = lax.all_gather(received, "rep", axis=0, tiled=True)
    summed_grad = (
        jnp.zeros(entity_table.shape, jnp.float32)
        .at[all_ids.reshape(-1)]
        .add(all_grads.reshape(-1, width))
    )
    updated = entity_table - learn_rate * summed_grad
    row_norms = jnp.sqrt(jnp.sum(updated * updated, 1) + norm_eps)
    local_norm = jnp.sum(row_norms)
    filter_total = lax.psum(filter_part, ("ent", "rep"))
    norm_total = lax.psum(local_norm, "ent")
    filter_grad = filter_total / (batch_rows * ent_count * rep_count)
    target = 0.25 * running_norm + 0.75 * norm_total / (entity_table.shape[0] * ent_count)
    new_table = jnp.where(
        (rare_flag == 1)[:, None], updated * (target / row_norms)[:, None], updated
    )
    return (new_table, filter_grad)


def solution(mesh):
    in_specs = (
        P("ent", None),
        P(),
        P(),
        P(),
        P(("ent", "rep"), None),
        P(("ent", "rep")),
        P(("ent", "rep")),
        P("ent"),
        P(),
    )
    out_specs = (P("ent", None), P())
    return jax.shard_map(body, mesh=mesh, in_specs=in_specs, out_specs=out_specs, check_vma=False)
```

profile of v0, /device:TPU:1, one launch (start us, length us, event | category | flops | bytes accessed | tf_op | source)
XLA Modules:
  0.0 538.2 jit_solution(8350565503353187962)
XLA Ops:
  7.2 0.7 reduce
  8.3 0.2 fusion.15
  8.5 0.7 fusion.22
  9.2 3.1 scatter_custom_fusion
  12.3 0.7 all_to_all.16
  13.1 18.4 %all-to-all-start = ((s32[128,1,4]{2,1,0:T(1,128)}), s32[128,1,4]{2,1,0:T(1,128)S(1)}, u32[]{:S(2)}, u32[]{:S(2)}) async-start(s32[128,1,4]{2,1,0:T(1,128)} %bitcast.4), calls=%async_computation | async-start | bytes 131072 | tf_op jit(solution)/shard_map/all_to_all | solution.py:83
  31.5 1.2 copy.117
  32.7 10.2 %all-to-all-done = s32[128,1,4]{2,1,0:T(1,128)S(1)} async-done(((s32[128,1,4]{2,1,0:T(1,128)}), s32[128,1,4]{2,1,0:T(1,128)S(1)}, u32[]{:S(2)}, u32[]{:S(2)}) %all-to-all-start) | async-done | bytes 2080 | tf_op jit(solution)/shard_map/all_to_all | solution.py:83
  43.1 0.5 copy-done.2
  43.6 1.6 gather_fusion
  45.1 0.9 reshape.144
  46.1 5.7 %all-to-all-start.1 = ((f32[128,4,200]{2,1,0:T(4,128)}), f32[128,4,200]{2,1,0:T(4,128)S(1)}, u32[]{:S(2)}, u32[]{:S(2)}) async-start(f32[128,4,200]{2,1,0:T(4,128)} %reshape.144), calls=%async_computation.1 | async-start | bytes 1048576 | tf_op jit(solution)/shard_map/all_to_all | solution.py:85
  51.8 0.5 all-gather.3.cloned.1.call-start
  52.3 0.2 copy.100
  52.6 0.8 gather_fusion.2
  53.6 17.8 %all-to-all-done.1 = f32[128,4,200]{2,1,0:T(4,128)S(1)} async-done(((f32[128,4,200]{2,1,0:T(4,128)}), f32[128,4,200]{2,1,0:T(4,128)S(1)}, u32[]{:S(2)}, u32[]{:S(2)}) %all-to-all-start.1) | async-done | bytes 409632 | tf_op jit(solution)/shard_map/all_to_all | solution.py:85
  71.4 0.2 reshape.133
  71.6 1.6 gather_fusion.1
  73.2 0.7 fusion.28
  74.1 7.1 %multiply_convert_fusion = (bf16[128,32,38,8]{0,1,3,2:T(8,128)(2,1)S(1)}, f32[128,32,38,8]{0,1,3,2:T(8,128)}) fusion(f32[32,1,3,3]{0,1,3,2:T(1,128)S(1)} %reshape.195, f32[128,1,40,10]{0,2,3,1:T(8,128)S(1)} %bitcast.46), kind=kOutput, calls=%fused_computation.9 | convolution fusion | flops 140705792 | bytes 7677056 | tf_op jit(solution)/shard_map/jvp()/conv_general_dilated | solution.py:19
  81.2 1.0 copy.105
  82.1 1.6 copy.123
  83.8 3.5 multiply_reduce_fusion.1
  87.2 0.3 fusion.8
  87.6 0.3 fusion.25
  87.9 0.4 fusion.4
  88.3 2.0 fusion.30
  90.4 2.6 fusion.1
  93.1 2.2 copy-done
  95.3 23.1 %fusion.29 = f32[128,1,40,10]{0,1,3,2:T(1,128)S(1)} fusion(f32[128,32,38,8]{0,1,3,2:T(8,128)S(1)} %fusion.1, f32[32,1,3,3]{0,1,3,2:T(1,128)S(1)} %reshape.195), kind=kOutput, calls=%fused_computation.68 | convolution fusion | flops 134479872 | bytes 5186688 | tf_op jit(solution)/shard_map/transpose(jvp())/conv_general_dilated | solution.py:19
  118.5 0.1 copy.114
  118.7 1.9 scatter_custom_fusion.1
  120.6 0.2 reshape.138
  120.7 26.3 %all_to_all.25 = f32[128,4,200]{2,1,0:T(4,128)S(1)} all-to-all(f32[128,4,200]{2,1,0:T(4,128)S(1)} %reshape.138), channel_id=1, replica_groups=mesh['ent'=128,'rep'=4] {'ent'}, dimensions={0} | all-to-all | bytes 819200 | tf_op jit(solution)/shard_map/all_to_all | solution.py:97
  147.0 1.0 copy.115
  148.7 8.4 %all-gather = s32[512,1,4]{0,2,1:T(4,128)S(1)} all-gather(s32[128,1,4]{0,2,1:T(4,128)S(1)} %copy.96), channel_id=2, replica_groups=mesh['ent'=128,'rep'=4] {'rep'}, dimensions={0}, use_global_device_ids=true | all-gather | bytes 10240 | tf_op jit(solution)/shard_map/all_gather | solution.py:98
  157.3 0.2 reshape.132
  157.5 9.4 %convolution_reduce_fusion = f32[32,3,3]{0,2,1:T(4,128)S(1)} fusion(f32[128,32,38,8]{0,1,3,2:T(8,128)} %copy-done, f32[128,1,40,10]{0,2,3,1:T(8,128)S(1)} %bitcast.47), kind=kOutput, calls=%fused_computation.20 | convolution fusion | flops 134479872 | bytes 5186688 | tf_op jit(solution)/shard_map/transpose(jvp())/conv_general_dilated | solution.py:19
  166.9 97.7 %psum.15 = f32[32,9]{0,1:T(8,128)S(1)} all-reduce(f32[32,9]{0,1:T(8,128)S(1)} %reshape.140), channel_id=1, replica_groups=mesh['ent'=128,'rep'=4] {'ent','rep'}, use_global_device_ids=true, to_apply=%region_10.11 | all-reduce | flops 288 | bytes 2304 | tf_op jit(solution)/shard_map/psum | solution.py:108
  264.6 2.0 copy.116
  266.6 1.8 reshape.187
  268.3 12.1 %scatter_custom_fusion.2 = f32[512,200]{1,0:T(8,128)S(1)} fusion(s32[2048]{0:T(1024)S(1)} %bitcast.53, f32[2048,200]{1,0:T(8,128)} %reshape.187, f32[]{:T(128)} %constant.16.clone.1), kind=kCustom, calls=%fused_computation.28 | custom fusion | flops 409600 | bytes 410112 | tf_op jit(solution)/shard_map/scatter-add | solution.py:103
  280.4 0.2 multiply_reduce_fusion
  280.6 0.6 sqrt_reduce_fusion
  281.2 0.6 broadcast_multiply_fusion.1
  281.8 247.5 %psum.14 = f32[]{:T(128)} all-reduce(f32[]{:T(128)} %sqrt_reduce_fusion), channel_id=1, replica_groups=mesh['ent'=128,'rep'=4] {'ent'}, use_global_device_ids=true, to_apply=%region_9.10 | all-reduce | flops 1 | bytes 8 | tf_op jit(solution)/shard_map/psum | solution.py:109
  529.9 0.2 multiply_select_fusion
  530.1 0.9 copy.119
  (59 shorter events, 1.3 us)
Async XLA Ops:
  8.0 44.3 %copy-start.5 = (bf16[822,200]{0,1:T(8,128)(2,1)S(1)}, bf16[822,200]{0,1:T(8,128)(2,1)}, u32[]{:S(2)}) copy-start(bf16[822,200]{0,1:T(8,128)(2,1)} %param.10) | copy-start | bytes 986404
  8.2 44.3 %copy-start.9 = (s32[128]{0:T(128)S(1)}, s32[128]{0:T(128)}, u32[]{:S(2)}) copy-start(s32[128]{0:T(128)} %param.15) | copy-start | bytes 1540
  8.5 45.1 %copy-start.6 = (f32[32,9]{0,1:T(8,128)S(1)}, f32[32,9]{0,1:T(8,128)}, u32[]{:S(2)}) copy-start(f32[32,9]{0,1:T(8,128)} %param.11) | copy-start | bytes 3460
  9.2 62.3 %copy-start.7 = (s32[320]{0:T(512)}, s32[320]{0:T(512)S(1)}, u32[]{:S(2)}) copy-start(s32[320]{0:T(512)S(1)} %fusion.22) | copy-start | bytes 3844
  13.1 29.9 %all-to-all-start = ((s32[128,1,4]{2,1,0:T(1,128)}), s32[128,1,4]{2,1,0:T(1,128)S(1)}, u32[]{:S(2)}, u32[]{:S(2)}) async-start(s32[128,1,4]{2,1,0:T(1,128)} %bitcast.4), calls=%async_computation | async-start | bytes 131072 | tf_op jit(solution)/shard_map/all_to_all | solution.py:83
  42.9 0.6 copy-start.2
  46.1 25.3 %all-to-all-start.1 = ((f32[128,4,200]{2,1,0:T(4,128)}), f32[128,4,200]{2,1,0:T(4,128)S(1)}, u32[]{:S(2)}, u32[]{:S(2)}) async-start(f32[128,4,200]{2,1,0:T(4,128)} %reshape.144), calls=%async_computation.1 | async-start | bytes 1048576 | tf_op jit(solution)/shard_map/all_to_all | solution.py:85
  51.8 212.8 %all-gather.3.cloned.1.call-start = ((), (), s32[]{:S(2)}) async-start(), calls=%async_computation.3 | async-start | bytes 2048000 | tf_op jit(solution)/shard_map/all_gather | solution.py:99
  83.8 4.1 copy-start.4
  83.8 4.5 copy-start.1
  87.5 2.8 slice-start
  88.3 2.1 slice-start.1
  93.1 2.2 copy-start
  95.3 53.4 %copy-start.8 = (s32[512]{0:T(512)S(1)}, s32[512]{0:T(512)}, u32[]{:S(2)}) copy-start(s32[512]{0:T(512)} %param.16) | copy-start | bytes 6148
  95.3 53.4 %copy-start.3 = (s32[128,1,4]{2,1,0:T(1,128)S(1)}, s32[128,1,4]{2,1,0:T(1,128)}, u32[]{:S(2)}) copy-start(s32[128,1,4]{2,1,0:T(1,128)} %copy-done.2) | copy-start | bytes 6148
Sparse Core Ops, SparseCore 0:
  148.1 28.8 all-gather.2
where the time goes:
time: 544 us; the launch traced here: 538 us
  blocking collectives  380 us (70%)
  matrix products  46 us (8%)
  waiting for transfers between devices  28 us (5%)
  local copies, waits for them, and re-layouts  25.1 us (5%)
  starting transfers between devices  24.6 us (5%)
  other arithmetic  18.4 us (3%)
  between operations  16.1 us (3%)
    psum x1, blocking collectives, body(): norm_total = lax.psum(local_norm, 'ent')  247 us
    psum x1, blocking collectives, body(): filter_total = lax.psum(filter_part, ('ent', 'rep'))  97.7 us
    conv_general_dilated x3, matrix products, conv_act(): lax.conv_general_dilated(stacked, kernel, (1, 1), 'VALID', precision=lax....  39.5 us
    all_to_all x1, blocking collectives, body(): lax.all_to_all(send_grads, 'ent', split_axis=0, concat_axis=0, tiled=True)  26.3 us
    all_to_all x1, starting transfers between devices, body(): lax.all_to_all(send_ids, 'ent', split_axis=0, concat_axis=0, tiled=True)  18.4 us
    all_to_all x1, waiting for transfers between devices, body(): lax.all_to_all(found_rows, 'ent', split_axis=0, concat_axis=0, tiled=True)  17.8 us
    scatter-add x1, other arithmetic, body(): summed_grad = jnp.zeros(entity_table.shape, jnp.float32).at[all_ids.resha...  12.1 us
  transfers between devices with their start and end apart: 3, of which 2 were waited for; matrix products, arithmetic and copies ran while one was open for 2% of the time, Pallas kernels for 0%

commit v1 on v0

--- a/solution.py
+++ b/solution.py
@@ -105,7 +105,7 @@
     updated = entity_table - learn_rate * summed_grad
     row_norms = jnp.sqrt(jnp.sum(updated * updated, 1) + norm_eps)
     local_norm = jnp.sum(row_norms)
-    filter_total = lax.psum(filter_part, ("ent", "rep"))
+    filter_total = lax.psum(lax.psum(filter_part, "ent"), "rep")
     norm_total = lax.psum(local_norm, "ent")
     filter_grad = filter_total / (batch_rows * ent_count * rep_count)
     target = 0.25 * running_norm + 0.75 * norm_total / (entity_table.shape[0] * ent_count)

time: 544 us -> 477 us (0.88)
  blocking collectives: 380 us -> 300 us
  waiting for transfers between devices: 28 us -> 38.1 us
    psum x1, blocking collectives: 97.7 us -> 7.85 us  [body(): filter_total = lax.psum(lax.psum(filter_part, 'ent'), 'rep')]
    all_gather x1, waiting for transfers between devices: 0.01 us -> 10.1 us  [body(): all_grads = lax.all_gather(received, 'rep', axis=0, tiled=True)]
    psum x1, blocking collectives: 247 us -> 257 us  [body(): norm_total = lax.psum(local_norm, 'ent')]
  transfers between devices with their start and end apart: 3 -> 3, of which waited for: 2 -> 3; matrix products, arithmetic and copies ran while one was open for 2% -> 3% of each run, Pallas kernels for 0% -> 0%
where the time goes in v1:
time: 477 us; the launch traced here: 468 us
  blocking collectives  300 us (63%)
  matrix products  46 us (10%)
  waiting for transfers between devices  38.1 us (8%)
  local copies, waits for them, and re-layouts  25.1 us (5%)
  starting transfers between devices  24.6 us (5%)
  other arithmetic  18.4 us (4%)
  between operations  16.1 us (3%)
    psum x1, blocking collectives, body(): norm_total = lax.psum(local_norm, 'ent')  257 us
    conv_general_dilated x3, matrix products, conv_act(): lax.conv_general_dilated(stacked, kernel, (1, 1), 'VALID', precision=lax....  39.5 us
    all_to_all x1, blocking collectives, body(): lax.all_to_all(send_grads, 'ent', split_axis=0, concat_axis=0, tiled=True)  26.3 us
    all_to_all x1, starting transfers between devices, body(): lax.all_to_all(send_ids, 'ent', split_axis=0, concat_axis=0, tiled=True)  18.4 us
    all_to_all x1, waiting for transfers between devices, body(): lax.all_to_all(found_rows, 'ent', split_axis=0, concat_axis=0, tiled=True)  17.8 us
    scatter-add x1, other arithmetic, body(): summed_grad = jnp.zeros(entity_table.shape, jnp.float32).at[all_ids.resha...  12.1 us
    all_to_all x1, waiting for transfers between devices, body(): lax.all_to_all(send_ids, 'ent', split_axis=0, concat_axis=0, tiled=True)  10.2 us
    all_gather x1, waiting for transfers between devices, body(): all_grads = lax.all_gather(received, 'rep', axis=0, tiled=True)  10.1 us
  transfers between devices with their start and end apart: 3, of which 3 were waited for; matrix products, arithmetic and copies ran while one was open for 3% of the time, Pallas kernels for 0%

profile of v1, /device:TPU:1, one launch (start us, length us, event | category | flops | bytes accessed | tf_op | source)
XLA Modules:
  0.0 468.3 jit_solution(6184904011701899252)
XLA Ops:
  7.2 0.7 reduce
  8.3 0.2 fusion.15
  8.5 0.7 fusion.22
  9.2 3.1 scatter_custom_fusion
  12.3 0.7 all_to_all.16
  13.1 18.4 %all-to-all-start = ((s32[128,1,4]{2,1,0:T(1,128)}), s32[128,1,4]{2,1,0:T(1,128)S(1)}, u32[]{:S(2)}, u32[]{:S(2)}) async-start(s32[128,1,4]{2,1,0:T(1,128)} %bitcast.4), calls=%async_computation | async-start | bytes 131072 | tf_op jit(solution)/shard_map/all_to_all | solution.py:83
  31.5 1.2 copy.117
  32.7 10.2 %all-to-all-done = s32[128,1,4]{2,1,0:T(1,128)S(1)} async-done(((s32[128,1,4]{2,1,0:T(1,128)}), s32[128,1,4]{2,1,0:T(1,128)S(1)}, u32[]{:S(2)}, u32[]{:S(2)}) %all-to-all-start) | async-done | bytes 2080 | tf_op jit(solution)/shard_map/all_to_all | solution.py:83
  43.1 0.5 copy-done.2
  43.6 1.6 gather_fusion
  45.1 0.9 reshape.144
  46.1 5.7 %all-to-all-start.1 = ((f32[128,4,200]{2,1,0:T(4,128)}), f32[128,4,200]{2,1,0:T(4,128)S(1)}, u32[]{:S(2)}, u32[]{:S(2)}) async-start(f32[128,4,200]{2,1,0:T(4,128)} %reshape.144), calls=%async_computation.1 | async-start | bytes 1048576 | tf_op jit(solution)/shard_map/all_to_all | solution.py:85
  51.8 0.5 all-gather.3.cloned.1.call-start
  52.3 0.2 copy.100
  52.6 0.8 gather_fusion.2
  53.6 17.8 %all-to-all-done.1 = f32[128,4,200]{2,1,0:T(4,128)S(1)} async-done(((f32[128,4,200]{2,1,0:T(4,128)}), f32[128,4,200]{2,1,0:T(4,128)S(1)}, u32[]{:S(2)}, u32[]{:S(2)}) %all-to-all-start.1) | async-done | bytes 409632 | tf_op jit(solution)/shard_map/all_to_all | solution.py:85
  71.4 0.2 reshape.133
  71.6 1.6 gather_fusion.1
  73.2 0.7 fusion.28
  74.1 7.1 %multiply_convert_fusion = (bf16[128,32,38,8]{0,1,3,2:T(8,128)(2,1)S(1)}, f32[128,32,38,8]{0,1,3,2:T(8,128)}) fusion(f32[32,1,3,3]{0,1,3,2:T(1,128)S(1)} %reshape.195, f32[128,1,40,10]{0,2,3,1:T(8,128)S(1)} %bitcast.46), kind=kOutput, calls=%fused_computation.9 | convolution fusion | flops 140705792 | bytes 7677056 | tf_op jit(solution)/shard_map/jvp()/conv_general_dilated | solution.py:19
  81.2 1.0 copy.105
  82.1 1.6 copy.123
  83.8 3.5 multiply_reduce_fusion.1
  87.2 0.3 fusion.8
  87.6 0.3 fusion.25
  87.9 0.4 fusion.4
  88.3 2.0 fusion.30
  90.4 2.6 fusion.1
  93.1 2.2 copy-done
  95.3 23.1 %fusion.29 = f32[128,1,40,10]{0,1,3,2:T(1,128)S(1)} fusion(f32[128,32,38,8]{0,1,3,2:T(8,128)S(1)} %fusion.1, f32[32,1,3,3]{0,1,3,2:T(1,128)S(1)} %reshape.195), kind=kOutput, calls=%fused_computation.68 | convolution fusion | flops 134479872 | bytes 5186688 | tf_op jit(solution)/shard_map/transpose(jvp())/conv_general_dilated | solution.py:19
  118.7 1.9 scatter_custom_fusion.1
  120.6 0.2 reshape.138
  120.7 26.3 %all_to_all.25 = f32[128,4,200]{2,1,0:T(4,128)S(1)} all-to-all(f32[128,4,200]{2,1,0:T(4,128)S(1)} %reshape.138), channel_id=1, replica_groups=mesh['ent'=128,'rep'=4] {'ent'}, dimensions={0} | all-to-all | bytes 819200 | tf_op jit(solution)/shard_map/all_to_all | solution.py:97
  147.0 1.0 copy.115
  148.7 8.4 %all-gather = s32[512,1,4]{0,2,1:T(4,128)S(1)} all-gather(s32[128,1,4]{0,2,1:T(4,128)S(1)} %copy.96), channel_id=2, replica_groups=mesh['ent'=128,'rep'=4] {'rep'}, dimensions={0}, use_global_device_ids=true | all-gather | bytes 10240 | tf_op jit(solution)/shard_map/all_gather | solution.py:98
  157.3 0.2 reshape.132
  157.5 9.4 %convolution_reduce_fusion = f32[32,3,3]{0,2,1:T(4,128)S(1)} fusion(f32[128,32,38,8]{0,1,3,2:T(8,128)} %copy-done, f32[128,1,40,10]{0,2,3,1:T(8,128)S(1)} %bitcast.47), kind=kOutput, calls=%fused_computation.20 | convolution fusion | flops 134479872 | bytes 5186688 | tf_op jit(solution)/shard_map/transpose(jvp())/conv_general_dilated | solution.py:19
  166.9 10.1 %all-gather.3.cloned.1.call-done = f32[512,4,200]{0,2,1:T(8,128)} async-done(((f32[128,4,200]{0,2,1:T(8,128)}), f32[512,4,200]{0,2,1:T(8,128)}) %all-gather.3.cloned.1.call-update) | async-done | bytes 1638416 | tf_op jit(solution)/shard_map/all_gather | solution.py:99
  177.0 2.0 copy.116
  179.0 1.8 reshape.187
  180.8 12.1 %scatter_custom_fusion.2 = f32[512,200]{1,0:T(8,128)S(1)} fusion(s32[2048]{0:T(1024)S(1)} %bitcast.53, f32[2048,200]{1,0:T(8,128)} %reshape.187, f32[]{:T(128)} %constant.16.clone.1), kind=kCustom, calls=%fused_computation.28 | custom fusion | flops 409600 | bytes 410112 | tf_op jit(solution)/shard_map/scatter-add | solution.py:103
  192.9 0.2 multiply_reduce_fusion
  193.0 0.6 sqrt_reduce_fusion
  193.6 257.4 %all-reduce.1 = (f32[]{:T(128)}, f32[32,9]{0,1:T(8,128)S(1)}) all-reduce(f32[]{:T(128)} %sqrt_reduce_fusion, f32[32,9]{0,1:T(8,128)S(1)} %reshape.140), channel_id=1, replica_groups=mesh['ent'=128,'rep'=4] {'ent'}, use_global_device_ids=true, to_apply=%region_9.10 | all-reduce | flops 289 | bytes 2312 | tf_op jit(solution)/shard_map/psum | solution.py:109
  451.7 0.2 multiply_select_fusion
  451.9 0.9 copy.119
  452.8 7.9 %psum.23 = f32[32,9]{0,1:T(8,128)S(1)} all-reduce(f32[32,9]{0,1:T(8,128)S(1)} %get-tuple-element.11), channel_id=1, replica_groups=mesh['ent'=128,'rep'=4] {'rep'}, use_global_device_ids=true, to_apply=%region_11.12 | all-reduce | flops 288 | bytes 2304 | tf_op jit(solution)/shard_map/psum | solution.py:108
  460.7 0.6 broadcast_multiply_fusion.1
  (59 shorter events, 1.4 us)
Async XLA Ops:
  8.0 44.3 %copy-start.5 = (bf16[822,200]{0,1:T(8,128)(2,1)S(1)}, bf16[822,200]{0,1:T(8,128)(2,1)}, u32[]{:S(2)}) copy-start(bf16[822,200]{0,1:T(8,128)(2,1)} %param.10) | copy-start | bytes 986404
  8.2 44.3 %copy-start.9 = (s32[128]{0:T(128)S(1)}, s32[128]{0:T(128)}, u32[]{:S(2)}) copy-start(s32[128]{0:T(128)} %param.15) | copy-start | bytes 1540
  8.5 45.1 %copy-start.6 = (f32[32,9]{0,1:T(8,128)S(1)}, f32[32,9]{0,1:T(8,128)}, u32[]{:S(2)}) copy-start(f32[32,9]{0,1:T(8,128)} %param.11) | copy-start | bytes 3460
  9.2 62.3 %copy-start.7 = (s32[320]{0:T(512)}, s32[320]{0:T(512)S(1)}, u32[]{:S(2)}) copy-start(s32[320]{0:T(512)S(1)} %fusion.22) | copy-start | bytes 3844
  13.1 29.9 %all-to-all-start = ((s32[128,1,4]{2,1,0:T(1,128)}), s32[128,1,4]{2,1,0:T(1,128)S(1)}, u32[]{:S(2)}, u32[]{:S(2)}) async-start(s32[128,1,4]{2,1,0:T(1,128)} %bitcast.4), calls=%async_computation | async-start | bytes 131072 | tf_op jit(solution)/shard_map/all_to_all | solution.py:83
  42.9 0.6 copy-start.2
  46.1 25.3 %all-to-all-start.1 = ((f32[128,4,200]{2,1,0:T(4,128)}), f32[128,4,200]{2,1,0:T(4,128)S(1)}, u32[]{:S(2)}, u32[]{:S(2)}) async-start(f32[128,4,200]{2,1,0:T(4,128)} %reshape.144), calls=%async_computation.1 | async-start | bytes 1048576 | tf_op jit(solution)/shard_map/all_to_all | solution.py:85
  51.8 125.2 %all-gather.3.cloned.1.call-start = ((), (), s32[]{:S(2)}) async-start(), calls=%async_computation.3 | async-start | bytes 2048000 | tf_op jit(solution)/shard_map/all_gather | solution.py:99
  83.8 4.1 copy-start.4
  83.8 4.5 copy-start.1
  87.5 2.8 slice-start
  88.3 2.1 slice-start.1
  93.1 2.2 copy-start
  95.3 53.4 %copy-start.8 = (s32[512]{0:T(512)S(1)}, s32[512]{0:T(512)}, u32[]{:S(2)}) copy-start(s32[512]{0:T(512)} %param.16) | copy-start | bytes 6148
  95.3 53.4 %copy-start.3 = (s32[128,1,4]{2,1,0:T(1,128)S(1)}, s32[128,1,4]{2,1,0:T(1,128)}, u32[]{:S(2)}) copy-start(s32[128,1,4]{2,1,0:T(1,128)} %copy-done.2) | copy-start | bytes 6148
Sparse Core Ops, SparseCore 0:
  148.1 28.8 all-gather.2
